TPU v7x, 32 devices: a whole 2x2x4 slice. The times are simulated.
32 devices in a mesh: groups: 2 (over y), ctx: 4 (over z), tm: 2 (over x), tp: 2 (over core).
Axes of the slice: x: 2, y: 2, z: 4, core: 2. Of those that a mesh axis runs over, the one named last changes fastest.
Arguments:
- tokens: bfloat16 [256, 8, 1024], P(('groups', 'tm'), 'ctx'), parts along dimension 0, may hold values from -6 to 6
- norm_gain: float32 [1024], replicated, may hold values from 0.1 to 1.9
- block_mask: int32 [4, 4, 4], P(('groups', 'tm'), 'ctx'), parts along dimension 0, may hold values from 0 to 1, as said below
- w_query: bfloat16 [1024, 1024], P('tm', 'tp'), may hold values from -1.25 to 1.25
- w_key: bfloat16 [1024, 1024], P('tm', 'tp'), may hold values from -1.25 to 1.25
- w_value: bfloat16 [1024, 1024], P('tm', 'tp'), may hold values from -0.1875 to 0.1875
- w_out: bfloat16 [1024, 1024], P('tp', 'tm'), may hold values from -0.1875 to 0.1875
- w_up: bfloat16 [1024, 2048], P('tm', 'tp'), may hold values from -0.1875 to 0.1875
- w_down: bfloat16 [2048, 1024], P('tp', 'tm'), may hold values from -0.125 to 0.125
- conv_weight: float32 [5, 1024], P(None, 'tp'), may hold values from -2.5 to 2.5
Outputs:
- denoised: bfloat16 [256, 8, 1024], P(('groups', 'tm'), 'ctx', 'tp'), parts along dimension 0
There are 2 independent parts, one for each index of `groups`. A program takes and returns all parts, laid end to end along the dimension named above; an argument that names none is the same for every part. Nothing has to cross between parts.
Inputs may be any that keep to these rules, and one draw needn't show every extreme that they name: block_mask[w, i, i] is 1 for every window w and block i.
All inputs are finite; a program needn't handle non-finite values.
Results may differ from a plain program's by a relative error of at most 0.0076.
Values may be sent and summed in bfloat16 or wider, within the bound.
A program may use at most 64 MiB of HBM per device.

v0:
```python
import jax
import jax.numpy as jnp
from jax import lax
from jax.sharding import PartitionSpec as P

HEAD_DIM = 64
KERNEL = 5


def from_behind(value, axis, steps):
    count = lax.axis_size(axis)
    first, last = (max(0, -steps), min(count, count - steps))
    return lax.ppermute(value, axis, [(source, source + steps) for source in range(first, last)])


def rms_norm(tokens, norm_gain):
    values = tokens.astype(jnp.float32)
    square = jnp.mean(values * values, axis=-1, keepdims=True)
    return (values * lax.rsqrt(square + 1e-05) * norm_gain).astype(jnp.bfloat16)


def on_device(
    tokens, norm_gain, block_mask, w_query, w_key, w_value, w_out, w_up, w_down, conv_weight
):
    frames_here, dancers_here, width = tokens.shape
    rows_here = frames_here * dancers_here
    normed_grid = rms_norm(tokens, norm_gain)
    normed = normed_grid.reshape(rows_here, width)
    pieces = (
        lax.all_gather(w_query, "tm", axis=0, tiled=True),
        lax.all_gather(w_key, "tm", axis=0, tiled=True),
        lax.all_gather(w_value, "tm", axis=0, tiled=True),
        lax.all_gather(w_up, "tm", axis=0, tiled=True),
    )
    query_sum, key_sum, value_sum, hidden = tuple(
        (jnp.dot(normed, piece_one, preferred_element_type=jnp.float32) for piece_one in pieces)
    )
    local_heads = query_sum.shape[1] // HEAD_DIM
    queries = query_sum.astype(jnp.bfloat16).reshape(rows_here, local_heads, HEAD_DIM)
    key_grid = key_sum.astype(jnp.bfloat16).reshape(
        frames_here, dancers_here, local_heads * HEAD_DIM
    )
    value_grid = value_sum.astype(jnp.bfloat16).reshape(
        frames_here, dancers_here, local_heads * HEAD_DIM
    )
    mask_row = block_mask[0, 0].astype(jnp.float32)
    cycle_blocks = mask_row.shape[0]
    key_piece = lax.all_gather(key_grid, "ctx", axis=1, tiled=True)
    value_piece = lax.all_gather(value_grid, "ctx", axis=1, tiled=True)
    count = key_piece.shape[1]
    block_ids = jnp.arange(count) // dancers_here
    picker = (block_ids[:, None] == jnp.arange(cycle_blocks)[None, :]).astype(jnp.float32)
    allowed_dancers = jnp.dot(picker, mask_row)
    peak_old = jnp.full((local_heads, rows_here), -1e30, jnp.float32)
    key_rows = key_piece.reshape(frames_here * count, local_heads, HEAD_DIM)
    value_rows = value_piece.reshape(frames_here * count, local_heads, HEAD_DIM)
    allowed = jnp.tile(allowed_dancers, frames_here)
    scores = (
        jnp.einsum("qhd,khd->hqk", queries, key_rows, preferred_element_type=jnp.float32) * 0.125
    )
    scores = jnp.where(allowed[None, None, :] > 0, scores, -1e30)
    peak_new = jnp.maximum(peak_old, jnp.max(scores, axis=-1))
    expo = jnp.exp(scores - peak_new[:, :, None]) * allowed[None, None, :]
    total_new = jnp.sum(expo, axis=-1)
    probs = expo.astype(jnp.bfloat16)
    mixed_new = jnp.einsum("hqk,khd->hqd", probs, value_rows, preferred_element_type=jnp.float32)
    attended = (
        (mixed_new / total_new[:, :, None])
        .transpose(1, 0, 2)
        .reshape(rows_here, local_heads * HEAD_DIM)
        .astype(jnp.bfloat16)
    )
    activated = jax.nn.gelu(hidden, approximate=True).astype(jnp.bfloat16)
    out_full, down_full = (
        lax.all_gather(w_out, "tm", axis=1, tiled=True),
        lax.all_gather(w_down, "tm", axis=1, tiled=True),
    )
    branches = jnp.dot(attended, out_full, preferred_element_type=jnp.float32)
    branches = branches + jnp.dot(activated, down_full, preferred_element_type=jnp.float32)
    mine = lax.psum_scatter(
        branches.astype(jnp.bfloat16), "tp", scatter_dimension=1, tiled=True
    ).astype(jnp.float32)
    features_here = mine.shape[1]
    first_feature = lax.axis_index("tp") * features_here
    normed_cols = lax.dynamic_slice_in_dim(normed_grid, first_feature, features_here, 2)
    padded = jnp.pad(normed_cols.astype(jnp.float32), ((4, 4), (0, 0), (0, 0)))
    extended = jnp.zeros((frames_here + 4, dancers_here, features_here), jnp.float32)
    for offset in range(KERNEL):
        extended = extended + conv_weight[offset] * padded[offset : offset + frames_here + 4]
    convolved = extended[2 : frames_here + 2]
    from_before = from_behind(extended[frames_here + 2 :], "tm", 1)
    from_after = from_behind(extended[0:2], "tm", -1)
    convolved = convolved.at[0:2].add(from_before)
    convolved = convolved.at[frames_here - 2 :].add(from_after)
    token_cols = lax.dynamic_slice_in_dim(tokens, first_feature, features_here, 2).astype(
        jnp.float32
    )
    result = token_cols + mine.reshape(frames_here, dancers_here, features_here) + convolved
    return result.astype(jnp.bfloat16)


def solution(mesh):
    placed = (
        P(("groups", "tm"), "ctx", None),
        P(),
        P(("groups", "tm"), "ctx", None),
        P("tm", "tp"),
        P("tm", "tp"),
        P("tm", "tp"),
        P("tp", "tm"),
        P("tm", "tp"),
        P("tp", "tm"),
        P(None, "tp"),
    )
    return jax.shard_map(
        on_device,
        mesh=mesh,
        in_specs=placed,
        out_specs=P(("groups", "tm"), "ctx", "tp"),
        check_vma=False,
    )
```

profile of v0, /device:TPU:0, one launch (start us, length us, event | category | flops | bytes accessed | tf_op | source)
XLA Modules:
  0.0 189.4 jit_solution(12623946930418223822)
XLA Ops:
  6.5 0.7 all-gather.7.cloned.1.call-update
  7.3 0.0 all-gather.9.cloned.1.call-start
  7.3 0.7 all-gather.9.cloned.1.call-update
  8.1 0.7 all-gather.11.cloned.1.call-update
  8.8 0.0 all-gather.17.cloned.1.call-start
  8.8 0.5 all-gather.17.cloned.1.call-update
  9.4 0.5 all-gather.15.cloned.1.call-update
  10.0 0.5 all-gather.13.cloned.1.call-update
  10.5 0.0 reduce-scatter.2.cloned.1.call-start
  10.6 0.3 fusion.15
  11.0 0.3 fusion.17
  11.3 0.1 reshape.127
  11.4 0.1 constant_dynamic-slice_fusion
  11.5 0.1 pad_convert_fusion
  11.7 0.2 convolution_bitcast_fusion.1
  11.9 0.1 broadcast_in_dim_tile.4
  12.0 1.0 fusion.26
  13.0 19.9 %all-gather.7.cloned.1.call-done = bf16[1024,512]{1,0:T(8,128)(2,1)} async-done(((bf16[512,512]{1,0:T(8,128)(2,1)}), bf16[1024,512]{1,0:T(8,128)(2,1)}) %all-gather.7.cloned.1.call-update) | async-done | bytes 1048592 | tf_op jit(solution)/shard_map/all_gather | solution.py:30
  32.9 1.5 convolution_convert_fusion.2
  34.5 0.1 copy.34
  34.6 21.2 %all-gather.9.cloned.1.call-done = bf16[1024,512]{1,0:T(8,128)(2,1)} async-done(((bf16[512,512]{1,0:T(8,128)(2,1)}), bf16[1024,512]{1,0:T(8,128)(2,1)}) %all-gather.9.cloned.1.call-update) | async-done | bytes 1048592 | tf_op jit(solution)/shard_map/all_gather | solution.py:31
  55.8 1.5 convolution_convert_fusion.1
  57.3 0.1 reshape.129
  57.4 15.5 %all_gather.26 = bf16[64,8,512]{2,0,1:T(8,128)(2,1)S(1)} all-gather(bf16[64,2,512]{2,0,1:T(8,128)(2,1)S(1)} %copy.35), channel_id=1, replica_groups=mesh['groups'=2,'ctx'=4,'tm'=2,'tp'=2] {'ctx'}, dimensions={1}, use_global_device_ids=true | all-gather | bytes 655360 | tf_op jit(solution)/shard_map/all_gather | solution.py:48
  72.8 0.3 copy.36
  73.1 0.5 reshape.130
  73.7 5.0 %all-gather.11.cloned.1.call-done = bf16[1024,512]{1,0:T(8,128)(2,1)} async-done(((bf16[512,512]{1,0:T(8,128)(2,1)}), bf16[1024,512]{1,0:T(8,128)(2,1)}) %all-gather.11.cloned.1.call-update) | async-done | bytes 1048592 | tf_op jit(solution)/shard_map/all_gather | solution.py:32
  78.6 1.5 convolution_convert_fusion
  80.2 0.1 reshape.131
  80.3 0.6 fusion
  80.9 15.5 %all_gather.28 = bf16[64,8,512]{2,0,1:T(8,128)(2,1)S(1)} all-gather(bf16[64,2,512]{2,0,1:T(8,128)(2,1)S(1)} %copy.38), channel_id=1, replica_groups=mesh['groups'=2,'ctx'=4,'tm'=2,'tp'=2] {'ctx'}, dimensions={1}, use_global_device_ids=true | all-gather | bytes 655360 | tf_op jit(solution)/shard_map/all_gather | solution.py:49
  96.3 0.3 copy.39
  96.6 1.5 reshape.132
  98.2 0.6 fusion.1
  98.8 0.6 copy-done.3
  99.4 0.9 fusion.5
  100.2 12.9 %all-gather.17.cloned.1.call-done = bf16[1024,1024]{1,0:T(8,128)(2,1)} async-done(((bf16[1024,512]{1,0:T(8,128)(2,1)}), bf16[1024,1024]{1,0:T(8,128)(2,1)}) %all-gather.17.cloned.1.call-update) | async-done | bytes 2097168 | tf_op jit(solution)/shard_map/all_gather | solution.py:76
  113.2 34.5 %all-gather.15.cloned.1.call-done = bf16[1024,1024]{1,0:T(8,128)(2,1)} async-done(((bf16[512,1024]{1,0:T(8,128)(2,1)}), bf16[1024,1024]{1,0:T(8,128)(2,1)}) %all-gather.15.cloned.1.call-update) | async-done | bytes 2097168 | tf_op jit(solution)/shard_map/all_gather | solution.py:33
  147.7 3.1 %fusion.30 = f32[128,1024]{1,0:T(8,128)S(1)} fusion(bf16[1024,1024]{1,0:T(8,128)(2,1)} %all-gather.17.cloned.1.call-done, bf16[128,1024]{1,0:T(8,128)(2,1)S(1)} %reshape.127, bf16[1024,1024]{1,0:T(8,128)(2,1)} %all-gather.15.cloned.1.call-done), kind=kOutput, calls=%fused_computation.45 | convolution fusion | flops 538050560 | bytes 4980736 | tf_op jit(solution)/shard_map/dot_general | solution.py:79
  150.8 19.6 %all-gather.13.cloned.1.call-done = bf16[512,1024]{1,0:T(8,128)(2,1)} async-done(((bf16[512,512]{1,0:T(8,128)(2,1)}), bf16[512,1024]{1,0:T(8,128)(2,1)}) %all-gather.13.cloned.1.call-update) | async-done | bytes 1048592 | tf_op jit(solution)/shard_map/all_gather | solution.py:75
  170.4 2.3 %fusion.3 = bf16[128,1024]{1,0:T(8,128)(2,1)} fusion(f32[128,1024]{1,0:T(8,128)S(1)} %fusion.30, bf16[128,512]{0,1:T(8,128)(2,1)S(1)} %bitcast.34, bf16[512,1024]{1,0:T(8,128)(2,1)} %all-gather.13.cloned.1.call-done), kind=kOutput, calls=%fused_computation.6 | convolution fusion | flops 134479872 | bytes 1966080 | tf_op jit(solution)/shard_map/dot_general | solution.py:78
  172.7 2.3 %collective-permute-start = (f32[2,2,512]{2,1,0:T(2,128)S(1)}, f32[2,2,512]{2,1,0:T(2,128)S(1)}, u32[]{:S(2)}, u32[]{:S(2)}) collective-permute-start(f32[2,2,512]{2,1,0:T(2,128)S(1)} %get-tuple-element.30), channel_id=1, source_target_pairs={{0,2},{1,3},{4,6},{5,7},{8,10},{9,11},{12,14},{13,15},{16,18},{17,... | collective-permute-start | bytes 24584 | tf_op jit(solution)/shard_map/ppermute | solution.py:13
  175.0 1.3 collective-permute-start.1
  176.3 0.0 collective-permute-done
  176.3 4.2 %collective-permute-done.1 = f32[2,2,512]{2,1,0:T(2,128)S(1)} collective-permute-done((f32[2,2,512]{2,1,0:T(2,128)S(1)}, f32[2,2,512]{2,1,0:T(2,128)S(1)}, u32[]{:S(2)}, u32[]{:S(2)}) %collective-permute-start.1) | collective-permute-done | bytes 8224 | tf_op jit(solution)/shard_map/ppermute | solution.py:13
  180.5 0.1 reduce-scatter.2.cloned.1.call-done
  180.6 1.1 reshape.136
  181.7 0.8 add_convert_fusion
  (31 shorter events, 0.3 us)
Async XLA Ops:
  6.5 4.0 %copy-start = (bf16[64,2,1024]{2,1,0:T(2,128)(2,1)S(1)}, bf16[64,2,1024]{2,1,0:T(2,128)(2,1)}, u32[]{:S(2)}) copy-start(bf16[64,2,1024]{2,1,0:T(2,128)(2,1)} %param.14) | copy-start | bytes 786436
  6.5 26.4 %all-gather.7.cloned.1.call-start = ((), (), s32[]{:S(2)}) async-start(), calls=%async_computation.1 | async-start | bytes 1572864 | tf_op jit(solution)/shard_map/all_gather | solution.py:30
  7.3 3.7 %copy-start.5 = (f32[1024]{0:T(1024)S(1)}, f32[1024]{0:T(1024)}, u32[]{:S(2)}) copy-start(f32[1024]{0:T(1024)} %param.15) | copy-start | bytes 12292
  7.3 48.5 %all-gather.9.cloned.1.call-start = ((), (), s32[]{:S(2)}) async-start(), calls=%async_computation.2 | async-start | bytes 1572864 | tf_op jit(solution)/shard_map/all_gather | solution.py:31
  8.0 70.6 %all-gather.11.cloned.1.call-start = ((), (), s32[]{:S(2)}) async-start(), calls=%async_computation.3 | async-start | bytes 1572864 | tf_op jit(solution)/shard_map/all_gather | solution.py:32
  8.8 104.4 %all-gather.17.cloned.1.call-start = ((), (), s32[]{:S(2)}) async-start(), calls=%async_computation.6 | async-start | bytes 3145728 | tf_op jit(solution)/shard_map/all_gather | solution.py:76
  9.3 2.3 %copy-start.4 = (f32[5,512]{1,0:T(8,128)S(1)}, f32[5,512]{1,0:T(8,128)}, u32[]{:S(2)}) copy-start(f32[5,512]{1,0:T(8,128)} %param.23) | copy-start | bytes 30724
  9.3 2.3 %copy-start.6 = (s32[1,1,4]{2,1,0:T(1,128)S(1)}, s32[1,1,4]{2,1,0:T(1,128)}, u32[]{:S(2)}) copy-start(s32[1,1,4]{2,1,0:T(1,128)} %param.16) | copy-start | bytes 52
  9.3 138.3 %all-gather.15.cloned.1.call-start = ((), (), s32[]{:S(2)}) async-start(), calls=%async_computation.5 | async-start | bytes 3145728 | tf_op jit(solution)/shard_map/all_gather | solution.py:33
  9.9 160.5 %all-gather.13.cloned.1.call-start = ((), (), s32[]{:S(2)}) async-start(), calls=%async_computation.4 | async-start | bytes 1572864 | tf_op jit(solution)/shard_map/all_gather | solution.py:75
  10.5 170.1 %reduce-scatter.2.cloned.1.call-start = ((), (), s32[]{:S(2)}) async-start(), calls=%async_computation.7 | async-start | bytes 393216 | tf_op jit(solution)/shard_map/reduce_scatter | solution.py:80
  98.1 1.2 copy-start.3
  150.7 21.9 %copy-start.2 = (f32[68,2,512]{2,1,0:T(2,128)S(1)}, f32[68,2,512]{2,1,0:T(2,128)}, u32[]{:S(2)}) copy-start(f32[68,2,512]{2,1,0:T(2,128)} %fusion.26) | copy-start | bytes 835588
  150.8 25.5 %slice-start = ((f32[68,2,512]{2,1,0:T(2,128)}), f32[64,2,512]{2,1,0:T(2,128)S(1)}, s32[]{:S(2)}) async-start(f32[68,2,512]{2,1,0:T(2,128)} %fusion.26), calls=%async_computation.8 | async-start | bytes 524288 | tf_op jit(solution)/shard_map/slice | solution.py:90
  150.8 30.9 %copy-start.1 = (bf16[64,2,1024]{2,1,0:T(2,128)(2,1)S(1)}, bf16[64,2,1024]{2,1,0:T(2,128)(2,1)}, u32[]{:S(2)}) copy-start(bf16[64,2,1024]{2,1,0:T(2,128)(2,1)} %param.14) | copy-start | bytes 786436
  172.7 3.6 %collective-permute-start = (f32[2,2,512]{2,1,0:T(2,128)S(1)}, f32[2,2,512]{2,1,0:T(2,128)S(1)}, u32[]{:S(2)}, u32[]{:S(2)}) collective-permute-start(f32[2,2,512]{2,1,0:T(2,128)S(1)} %get-tuple-element.30), channel_id=1, source_target_pairs={{0,2},{1,3},{4,6},{5,7},{8,10},{9,11},{12,14},{13,15},{16,18},{17,... | collective-permute-start | bytes 24584 | tf_op jit(solution)/shard_map/ppermute | solution.py:13
  175.0 5.5 %collective-permute-start.1 = (f32[2,2,512]{2,1,0:T(2,128)S(1)}, f32[2,2,512]{2,1,0:T(2,128)S(1)}, u32[]{:S(2)}, u32[]{:S(2)}) collective-permute-start(f32[2,2,512]{2,1,0:T(2,128)S(1)} %get-tuple-element.29), channel_id=1, source_target_pairs={{2,0},{3,1},{6,4},{7,5},{10,8},{11,9},{14,12},{15,13},{18,16},{19,... | collective-permute-start | bytes 24584 | tf_op jit(solution)/shard_map/ppermute | solution.py:13
Sparse Core Ops, SparseCore 0:
  8.9 23.9 all-gather.6
  34.5 21.2 all-gather.8
  57.3 21.2 all-gather.10
  80.0 33.0 all-gather.16
  114.5 33.0 all-gather.14
  149.1 21.2 all-gather.12
  172.8 7.7 reduce-scatter.1
where the time goes:
time: 190 us; the launch traced here: 189 us
  waiting for transfers between devices  121 us (64%)
  blocking collectives  30.9 us (16%)
  between operations  13.8 us (7%)
  matrix products  11.6 us (6%)
  local copies, waits for them, and re-layouts  4.94 us (3%)
  starting transfers between devices  3.77 us (2%)
  other arithmetic  3.36 us (2%)
    all_gather x1, waiting for transfers between devices, on_device(): lax.all_gather(w_up, 'tm', axis=0, tiled=True)  34.5 us
    all_gather x1, waiting for transfers between devices, on_device(): lax.all_gather(w_key, 'tm', axis=0, tiled=True)  21.2 us
    all_gather x1, waiting for transfers between devices, on_device(): lax.all_gather(w_query, 'tm', axis=0, tiled=True)  19.9 us
    all_gather x1, waiting for transfers between devices, on_device(): lax.all_gather(w_out, 'tm', axis=1, tiled=True)  19.6 us
    all_gather x1, blocking collectives, on_device(): key_piece = lax.all_gather(key_grid, 'ctx', axis=1, tiled=True)  15.5 us
    all_gather x1, blocking collectives, on_device(): value_piece = lax.all_gather(value_grid, 'ctx', axis=1, tiled=True)  15.5 us
    all_gather x1, waiting for transfers between devices, on_device(): lax.all_gather(w_down, 'tm', axis=1, tiled=True)  12.9 us
    all_gather x1, waiting for transfers between devices, on_device(): lax.all_gather(w_value, 'tm', axis=0, tiled=True)  4.95 us
  transfers between devices with their start and end apart: 9, of which 8 were waited for; matrix products, arithmetic and copies ran while one was open for 8% of the time, Pallas kernels for 0%

commit v1 on v0

--- a/solution.py
+++ b/solution.py
@@ -1,6 +1,10 @@
+import functools
+
 import jax
 import jax.numpy as jnp
 from jax import lax
+from jax.experimental import pallas as pl
+from jax.experimental.pallas import tpu as pltpu
 from jax.sharding import PartitionSpec as P
 
 HEAD_DIM = 64
@@ -99,7 +103,462 @@
     return result.astype(jnp.bfloat16)
 
 
+MESH = pl.DeviceIdType.MESH
+
+
+def normalised(values, gain):
+    values = values.astype(jnp.float32)
+    square = jnp.mean(values * values, axis=-1, keepdims=True)
+    return (values * lax.rsqrt(square + 1e-05) * gain).astype(jnp.bfloat16)
+
+
+def layer_kernel(
+    n_ctx,
+    frame,
+    mask_ref,
+    tokens_ref,
+    gain_ref,
+    conv_ref,
+    wq_ref,
+    wk_ref,
+    wv_ref,
+    wup_ref,
+    wout_ref,
+    wdown_ref,
+    out_ref,
+    tok_all,
+    normed,
+    halo,
+    halo_normed,
+    bias,
+    w_in,
+    w_back,
+    qkv,
+    feats,
+    theirs,
+    sibling,
+    mine,
+    summed,
+    arrived,
+    extended,
+    local_sem,
+    tok_send,
+    tok_recv,
+    fwd_send,
+    fwd_recv,
+    bias_send,
+    bias_recv,
+    x_send,
+    x_recv,
+    y_send,
+    y_recv,
+    halo_sem,
+    sib_send,
+    sib_recv,
+    red_send,
+    red_recv,
+):
+    g = lax.axis_index("groups")
+    c = lax.axis_index("ctx")
+    i = lax.axis_index("tm")
+    j = lax.axis_index("tp")
+    rows, width = tokens_ref.shape
+    half_rows = rows // 2
+    depth = wq_ref.shape[0]
+    part = depth // 2
+    hw = wq_ref.shape[1] // n_ctx
+    fw = wup_ref.shape[1] // n_ctx
+    cols = out_ref.shape[1]
+    heads = hw // HEAD_DIM
+    to_x = {"tm": 1 - i}
+    to_y = {"groups": 1 - g}
+    to_tp = {"tp": 1 - j}
+
+    def ahead(step):
+        return lax.rem(c + step, n_ctx)
+
+    def behind(step):
+        return lax.rem(c + n_ctx - step, n_ctx)
+
+    pieces = []
+    for block in range(n_ctx):
+        term = (mask_ref[0, block].astype(jnp.float32) - 1.0) * 1e30
+        pieces.append(jnp.full((8, rows), term, jnp.float32))
+    bias[c] = jnp.concatenate(pieces, axis=1)
+
+    barrier = pltpu.get_barrier_semaphore()
+    for peer in (to_x, to_y, to_tp):
+        pl.semaphore_signal(barrier, inc=1, device_id=peer, device_id_type=MESH)
+    for step in range(1, n_ctx):
+        pl.semaphore_signal(
+            barrier, inc=1, device_id={"ctx": ahead(step)}, device_id_type=MESH
+        )
+
+    def rows_at(start, size):
+        return pl.ds(pl.multiple_of(start, 16), size)
+
+    def cols_at(start, size):
+        return pl.ds(pl.multiple_of(start, 128), size)
+
+    def slices(first, count, owner):
+        out = []
+        for index, ref in enumerate((wq_ref, wk_ref, wv_ref)):
+            out.append(
+                (
+                    ref.at[rows_at(first * depth // 2, count * part), cols_at(c * hw, hw)],
+                    w_in.at[
+                        rows_at(owner * depth + first * part, count * part),
+                        index * hw : (index + 1) * hw,
+                    ],
+                )
+            )
+        out.append(
+            (
+                wup_ref.at[rows_at(first * part, count * part), cols_at(c * fw, fw)],
+                w_in.at[
+                    rows_at(owner * depth + first * part, count * part),
+                    3 * hw : 3 * hw + fw,
+                ],
+            )
+        )
+        out.append(
+            (
+                wout_ref.at[rows_at(c * hw + first * (hw // 2), count * (hw // 2)), :],
+                w_back.at[
+                    rows_at(first * (hw // 2), count * (hw // 2)),
+                    cols_at(owner * cols, cols),
+                ],
+            )
+        )
+        out.append(
+            (
+                wdown_ref.at[rows_at(c * fw + first * (fw // 2), count * (fw // 2)), :],
+                w_back.at[
+                    rows_at(hw + first * (fw // 2), count * (fw // 2)),
+                    cols_at(owner * cols, cols),
+                ],
+            )
+        )
+        return out
+
+    local = [
+        pltpu.make_async_copy(source, target, local_sem.at[index])
+        for index, (source, target) in enumerate(slices(0, 2, i))
+    ]
+    local.append(
+        pltpu.make_async_copy(
+            tokens_ref, tok_all.at[rows_at(c * rows, rows)], local_sem.at[6]
+        )
+    )
+    for copy in local:
+        copy.start()
+    pl.semaphore_wait(barrier, n_ctx + 2)
+
+    def remote(source, target, send, recv, peer):
+        return pltpu.make_async_remote_copy(
+            src_ref=source,
+            dst_ref=target,
+            send_sem=send,
+            recv_sem=recv,
+            device_id=peer,
+            device_id_type=MESH,
+        )
+
+    x_out = [
+        remote(source, target, x_send.at[index], x_recv.at[index], to_x)
+        for index, (source, target) in enumerate(slices(g, 1, i))
+    ]
+    x_in = [
+        remote(source, target, x_send.at[index], x_recv.at[index], to_x)
+        for index, (source, target) in enumerate(slices(g, 1, 1 - i))
+    ]
+    halo_copy = remote(
+        tokens_ref.at[rows_at((1 - i) * (rows - 16), 16)],
+        halo,
+        halo_sem.at[0],
+        halo_sem.at[1],
+        to_x,
+    )
+
+    def token_half(block, half):
+        return tok_all.at[rows_at(block * rows + half * half_rows, half_rows)]
+
+    tok_out, tok_in, fwd_out, fwd_in, bias_out, bias_in = [], [], [], [], [], []
+    for step in range(1, n_ctx):
+        peer = {"ctx": ahead(step)}
+        at = step - 1
+        own_half = tokens_ref.at[rows_at(j * half_rows, half_rows)]
+        tok_out.append(
+            remote(own_half, token_half(c, j), tok_send.at[at], tok_recv.at[at], peer)
+        )
+        source = behind(step)
+        tok_in.append(
+            remote(own_half, token_half(source, j), tok_send.at[at], tok_recv.at[at], peer)
+        )
+        fwd_out.append(
+            remote(
+                token_half(source, j), token_half(source, j), fwd_send.at[at], fwd_recv.at[at], to_tp
+            )
+        )
+        fwd_in.append(
+            remote(
+                token_half(source, 1 - j),
+                token_half(source, 1 - j),
+                fwd_send.at[at],
+                fwd_recv.at[at],
+                to_tp,
+            )
+        )
+        bias_out.append(remote(bias.at[c], bias.at[c], bias_send.at[at], bias_recv.at[at], peer))
+        bias_in.append(
+            remote(bias.at[source], bias.at[source], bias_send.at[at], bias_recv.at[at], peer)
+        )
+
+    def y_regions(half):
+        other = 1 - i
+        return [
+            w_in.at[rows_at(other * depth + half * part, part), 0 : 3 * hw],
+            w_in.at[rows_at(other * depth + half * part, part), 3 * hw : 3 * hw + fw],
+            w_back.at[rows_at(half * (hw // 2), hw // 2), cols_at(other * cols, cols)],
+            w_back.at[rows_at(hw + half * (fw // 2), fw // 2), cols_at(other * cols, cols)],
+        ]
+
+    y_out = [
+        remote(region, region, y_send.at[index], y_recv.at[index], to_y)
+        for index, region in enumerate(y_regions(g))
+    ]
+    y_in = [
+        remote(region, region, y_send.at[index], y_recv.at[index], to_y)
+        for index, region in enumerate(y_regions(1 - g))
+    ]
+
+    for copy in tok_out:
+        copy.start()
+    for copy in x_out[:4]:
+        copy.start()
+    halo_copy.start()
+    for copy in x_out[4:]:
+        copy.start()
+    for copy in bias_out:
+        copy.start()
+
+    gain = gain_ref[...]
+
+    def norm_block(block):
+        at = rows_at(block * rows, rows)
+        normed[at, :] = normalised(tok_all[at, :], gain)
+
+    local[6].wait()
+    norm_block(c)
+
+    tok_in[0].wait_recv()
+    fwd_out[0].start()
+    for copy in x_in[:3]:
+        copy.wait_recv()
+    y_out[0].start()
+    for at in range(1, n_ctx - 1):
+        tok_in[at].wait_recv()
+        fwd_out[at].start()
+        fwd_in[at - 1].wait_recv()
+        norm_block(behind(at))
+    x_in[3].wait_recv()
+    y_out[1].start()
+    fwd_in[n_ctx - 2].wait_recv()
+    norm_block(behind(n_ctx - 1))
+
+    for copy in local[:4]:
+        copy.wait()
+    y_in[0].wait_recv()
+
+    @pl.loop(0, n_ctx)
+    def _(block):
+        at = rows_at(block * rows, rows)
+        qkv[at, :] = jnp.dot(
+            normed[at, :], w_in[:, 0 : 3 * hw], preferred_element_type=jnp.float32
+        ).astype(jnp.bfloat16)
+
+    x_in[4].wait_recv()
+    y_out[2].start()
+    x_in[5].wait_recv()
+    y_out[3].start()
+    for copy in bias_in:
+        copy.wait_recv()
+
+    @pl.loop(0, n_ctx)
+    def _(block):
+        at = rows_at(block * rows, rows)
+        outs = []
+        for head in range(heads):
+            low = head * HEAD_DIM
+            query = qkv[at, low : low + HEAD_DIM]
+            key = qkv[:, hw + low : hw + low + HEAD_DIM]
+            value = qkv[:, 2 * hw + low : 2 * hw + low + HEAD_DIM]
+            scores = lax.dot_general(
+                query, key, (((1,), (1,)), ((), ())), preferred_element_type=jnp.float32
+            )
+            scores = scores * 0.125 + bias[block][0:1, :]
+            peak = jnp.max(scores, axis=-1, keepdims=True)
+            expo = jnp.exp(scores - peak)
+            total = jnp.sum(expo, axis=-1, keepdims=True)
+            mixed = jnp.dot(
+                expo.astype(jnp.bfloat16), value, preferred_element_type=jnp.float32
+            )
+            outs.append(mixed / total)
+        feats[at, 0:hw] = jnp.concatenate(outs, axis=1).astype(jnp.bfloat16)
+
+    y_in[1].wait_recv()
+
+    @pl.loop(0, n_ctx)
+    def _(block):
+        at = rows_at(block * rows, rows)
+        hidden = jnp.dot(
+            normed[at, :], w_in[:, 3 * hw : 3 * hw + fw], preferred_element_type=jnp.float32
+        )
+        feats[at, hw : hw + fw] = jax.nn.gelu(hidden, approximate=True).astype(jnp.bfloat16)
+
+    for copy in local[4:6]:
+        copy.wait()
+    y_in[2].wait_recv()
+    y_in[3].wait_recv()
+
+    order = list(range(1, n_ctx)) + [0]
+    sib_out, sib_in = [], []
+    for index, step in enumerate(order):
+        at = rows_at(ahead(step) * rows, rows)
+        copy = remote(
+            theirs.at[at], sibling.at[at], sib_send.at[index], sib_recv.at[index], to_tp
+        )
+        sib_out.append(copy)
+        theirs[at, :] = jnp.dot(
+            feats[at, :], w_back[:, cols_at((1 - j) * cols, cols)], preferred_element_type=jnp.float32
+        ).astype(jnp.bfloat16)
+        copy.start()
+    for index, step in enumerate(order):
+        at = rows_at(ahead(step) * rows, rows)
+        mine[at, :] = jnp.dot(
+            feats[at, :], w_back[:, cols_at(j * cols, cols)], preferred_element_type=jnp.float32
+        )
+    red = []
+    for index, step in enumerate(order[:-1]):
+        at = rows_at(ahead(step) * rows, rows)
+        sib_out[index].wait_recv()
+        summed[step - 1] = (mine[at, :] + sibling[at, :].astype(jnp.float32)).astype(jnp.bfloat16)
+        copy = remote(
+            summed.at[step - 1],
+            arrived.at[step - 1],
+            red_send.at[step - 1],
+            red_recv.at[step - 1],
+            {"ctx": ahead(step)},
+        )
+        copy.start()
+        red.append(copy)
+
+    halo_copy.wait_recv()
+    halo_normed[...] = normalised(halo[...], gain)
+    edge = halo_normed[:, cols_at(j * cols, cols)].astype(jnp.float32)
+    own = rows_at(c * rows, rows)
+    my_cols = cols_at(j * cols, cols)
+    reach = KERNEL // 2
+    before = jnp.where(i == 1, edge[8:16], 0.0)
+    after = jnp.where(i == 0, edge[0:8], 0.0)
+    extended[0:8, :] = before
+    extended[8 : 8 + rows, :] = normed[own, my_cols].astype(jnp.float32)
+    extended[8 + rows : 16 + rows, :] = after
+    base = tokens_ref[:, my_cols].astype(jnp.float32)
+    for tap in range(KERNEL):
+        shift = 8 + (tap - reach) * frame
+        base = base + conv_ref[tap : tap + 1, :] * extended[shift : shift + rows, :]
+    sib_out[n_ctx - 1].wait_recv()
+    base = base + mine[own, :] + sibling[own, :].astype(jnp.float32)
+    for copy in red:
+        copy.wait_recv()
+    for step in range(n_ctx - 1):
+        base = base + arrived[step].astype(jnp.float32)
+    out_ref[...] = base.astype(out_ref.dtype)
+
+    for copy in tok_out + x_out + [halo_copy] + bias_out + fwd_out + y_out + sib_out + red:
+        copy.wait_send()
+
+
+def in_one_kernel(
+    n_ctx, tokens, norm_gain, block_mask, w_query, w_key, w_value, w_out, w_up, w_down, conv_weight
+):
+    frames_here, dancers_here, width = tokens.shape
+    rows = frames_here * dancers_here
+    cols = w_out.shape[1]
+    hw = w_query.shape[1] // n_ctx
+    fw = w_up.shape[1] // n_ctx
+    depth = w_query.shape[0]
+    every = n_ctx * rows
+    bf16, f32 = jnp.bfloat16, jnp.float32
+    vmem = pl.BlockSpec(memory_space=pltpu.VMEM)
+    hbm = pl.BlockSpec(memory_space=pl.ANY)
+    dma = pltpu.SemaphoreType.DMA
+    out = pl.pallas_call(
+        functools.partial(layer_kernel, n_ctx, dancers_here),
+        out_shape=jax.ShapeDtypeStruct((rows, cols), bf16),
+        in_specs=[pl.BlockSpec(memory_space=pltpu.SMEM)] + [vmem] * 3 + [hbm] * 6,
+        out_specs=vmem,
+        scratch_shapes=[
+            pltpu.VMEM((every, width), bf16),
+            pltpu.VMEM((every, width), bf16),
+            pltpu.VMEM((16, width), bf16),
+            pltpu.VMEM((16, width), bf16),
+            pltpu.VMEM((n_ctx, 8, every), f32),
+            pltpu.VMEM((2 * depth, 3 * hw + fw), bf16),
+            pltpu.VMEM((hw + fw, 2 * cols), bf16),
+            pltpu.VMEM((every, 3 * hw), bf16),
+            pltpu.VMEM((every, hw + fw), bf16),
+            pltpu.VMEM((every, cols), bf16),
+            pltpu.VMEM((every, cols), bf16),
+            pltpu.VMEM((every, cols), f32),
+            pltpu.VMEM((n_ctx - 1, rows, cols), bf16),
+            pltpu.VMEM((n_ctx - 1, rows, cols), bf16),
+            pltpu.VMEM((rows + 16, cols), f32),
+            dma((7,)),
+            dma((n_ctx - 1,)),
+            dma((n_ctx - 1,)),
+            dma((n_ctx - 1,)),
+            dma((n_ctx - 1,)),
+            dma((n_ctx - 1,)),
+            dma((n_ctx - 1,)),
+            dma((6,)),
+            dma((6,)),
+            dma((4,)),
+            dma((4,)),
+            dma((2,)),
+            dma((n_ctx,)),
+            dma((n_ctx,)),
+            dma((n_ctx - 1,)),
+            dma((n_ctx - 1,)),
+        ],
+        compiler_params=pltpu.CompilerParams(
+            collective_id=0, has_side_effects=True, vmem_limit_bytes=40 << 20
+        ),
+    )(
+        block_mask[0],
+        tokens.reshape(rows, width),
+        norm_gain[None],
+        conv_weight,
+        w_query,
+        w_key,
+        w_value,
+        w_up,
+        w_out,
+        w_down,
+    )
+    return out.reshape(frames_here, dancers_here, cols)
+
+
 def solution(mesh):
+    def body(tokens, norm_gain, block_mask, w_query, *rest):
+        n_ctx = mesh.shape["ctx"]
+        pairs = all(mesh.shape[axis] == 2 for axis in ("groups", "tm", "tp"))
+        split = w_query.shape[1] % (128 * n_ctx) == 0 and tokens.shape[1] * (KERNEL // 2) <= 8
+        if pairs and split and n_ctx > 2:
+            return in_one_kernel(n_ctx, tokens, norm_gain, block_mask, w_query, *rest)
+        return on_device(tokens, norm_gain, block_mask, w_query, *rest)
+
     placed = (
         P(("groups", "tm"), "ctx", None),
         P(),
@@ -113,7 +572,7 @@
         P(None, "tp"),
     )
     return jax.shard_map(
-        on_device,
+        body,
         mesh=mesh,
         in_specs=placed,
         out_specs=P(("groups", "tm"), "ctx", "tp"),

time: 190 us -> 51.6 us (0.27)
  waiting for transfers between devices: 121 us -> 0 us
  Pallas kernels: 0 us -> 42.3 us
  blocking collectives: 30.9 us -> 0 us
  between operations: 13.8 us -> 0.04 us
  matrix products: 11.6 us -> 0 us
  local copies, waits for them, and re-layouts: 4.94 us -> 8.8 us
  starting transfers between devices: 3.77 us -> 0 us
  other arithmetic: 3.36 us -> 0 us
    all_gather x6 -> x0, waiting for transfers between devices: 113 us -> none  [the longest x1 34.5 us: on_device(): lax.all_gather(w_up, 'tm', axis=0, tiled=True)]
    pallas_call x0 -> x1, Pallas kernels: none -> 42.3 us  [in_one_kernel(): pl.pallas_call(functools.partial(layer_kernel, n_ctx, dancers_here), out_...]
    all_gather x2 -> x0, blocking collectives: 30.9 us -> none  [the longest x1 15.5 us: on_device(): key_piece = lax.all_gather(key_grid, 'ctx', axis=1, tiled=True)]
    dot_general x8 -> x0, matrix products: 11.6 us -> none  [the longest x3 4.59 us: on_device(): jnp.dot(normed, piece_one, preferred_element_type=jnp.float32)]
    unnamed x14 -> x18, local copies, waits for them, and re-layouts: 0.63 us -> 6.98 us
    ppermute x2 -> x0, waiting for transfers between devices: 4.23 us -> none  [from_behind(): lax.ppermute(value, axis, [(source, source + steps) for source in range(f...]
    unnamed x7 -> x0, waiting for transfers between devices: 3.68 us -> none
    ppermute x2 -> x0, starting transfers between devices: 3.54 us -> none  [from_behind(): lax.ppermute(value, axis, [(source, source + steps) for source in range(f...]
  transfers between devices with their start and end apart: 9 -> 0, of which waited for: 8 -> 0; matrix products, arithmetic and copies ran while one was open for 8% -> 0% of each run, Pallas kernels for 0% -> 0%
where the time goes in v1:
time: 51.6 us; the launch traced here: 51.1 us
  Pallas kernels  42.3 us (82%)
  local copies, waits for them, and re-layouts  8.8 us (17%)
    pallas_call x1, Pallas kernels, in_one_kernel(): pl.pallas_call(functools.partial(layer_kernel, n_ctx, dancers_here), out_...  42.3 us
    unnamed x18, local copies, waits for them, and re-layouts  6.98 us
    reshape x1, local copies, waits for them, and re-layouts, in_one_kernel(): tokens.reshape(rows, width)  1.11 us

profile of v1, /device:TPU:0, one launch (start us, length us, event | category | flops | bytes accessed | tf_op | source)
XLA Modules:
  0.0 51.1 jit_solution(13635478862224192577)
XLA Ops:
  0.0 0.0 copy-start.2
  0.0 0.0 copy-start.8
  0.0 1.1 %reshape.6.tokens_ref = bf16[128,1024]{1,0:T(8,128)(2,1)S(1)} reshape(bf16[64,2,1024]{2,1,0:T(2,128)(2,1)} %param.10) | data formatting | bytes 524288 | tf_op jit(solution)/shard_map/reshape | solution.py:540
  1.1 0.0 copy-done.2
  1.1 0.0 copy-done.8
  1.1 0.0 copy-start
  1.1 1.2 %copy-done = bf16[512,1024]{1,0:T(8,128)(2,1)S(1)} copy-done((bf16[512,1024]{1,0:T(8,128)(2,1)S(1)}, bf16[512,1024]{1,0:T(8,128)(2,1)}, u32[]{:S(2)}) %copy-start) | copy-done | bytes 1048600
  2.4 0.0 copy-start.1
  2.4 1.2 %copy-done.1 = bf16[1024,512]{1,0:T(8,128)(2,1)S(1)} copy-done((bf16[1024,512]{1,0:T(8,128)(2,1)S(1)}, bf16[1024,512]{1,0:T(8,128)(2,1)}, u32[]{:S(2)}) %copy-start.1) | copy-done | bytes 1048600
  3.6 0.0 copy-start.3
  3.6 1.0 %copy-done.3 = bf16[512,512]{1,0:T(8,128)(2,1)S(1)} copy-done((bf16[512,512]{1,0:T(8,128)(2,1)S(1)}, bf16[512,512]{1,0:T(8,128)(2,1)}, u32[]{:S(2)}) %copy-start.3) | copy-done | bytes 524312
  4.6 0.0 copy-start.4
  4.6 1.0 %copy-done.4 = bf16[512,512]{1,0:T(8,128)(2,1)S(1)} copy-done((bf16[512,512]{1,0:T(8,128)(2,1)S(1)}, bf16[512,512]{1,0:T(8,128)(2,1)}, u32[]{:S(2)}) %copy-start.4) | copy-done | bytes 524312
  5.7 0.0 copy-start.5
  5.7 1.0 %copy-done.5 = bf16[512,512]{1,0:T(8,128)(2,1)S(1)} copy-done((bf16[512,512]{1,0:T(8,128)(2,1)S(1)}, bf16[512,512]{1,0:T(8,128)(2,1)}, u32[]{:S(2)}) %copy-start.5) | copy-done | bytes 524312
  6.7 0.0 copy-start.6
  6.7 0.7 %copy-done.6 = f32[5,512]{1,0:T(8,128)S(1)} copy-done((f32[5,512]{1,0:T(8,128)S(1)}, f32[5,512]{1,0:T(8,128)}, u32[]{:S(2)}) %copy-start.6) | copy-done | bytes 10264
  7.4 0.0 copy-start.7
  7.4 0.7 %copy-done.7 = f32[1024]{0:T(1024)S(1)} copy-done((f32[1024]{0:T(1024)S(1)}, f32[1024]{0:T(1024)}, u32[]{:S(2)}) %copy-start.7) | copy-done | bytes 4120
  8.1 42.3 %shard_map.100 = bf16[128,512]{1,0:T(8,128)(2,1)S(1)} custom-call(s32[1,4]{1,0:T(1,128)S(1)} %bitcast.3, bf16[128,1024]{1,0:T(8,128)(2,1)S(1)} %reshape.6.tokens_ref, f32[1,1024]{1,0:T(1,128)S(1)} %bitcast.2, f32[5,512]{1,0:T(8,128)S(1)} %copy-done.6, bf16[512,512]{1,0:T(8,128)(2,1)S(1)} %copy-done.2, bf16[512,512]{1,0:T(8,128)(2,1)S(1)} %copy-done.3, ...), custom_call_target="tpu_custom_call" | custom-call | tf_op jit(solution)/shard_map/pallas_call | solution.py:497
  50.4 0.7 %reshape.7 = bf16[64,2,512]{2,1,0:T(2,128)(2,1)} reshape(bf16[128,512]{1,0:T(8,128)(2,1)S(1)} %shard_map.100) | data formatting | bytes 262144 | tf_op jit(solution)/shard_map/reshape | solution.py:550
Async XLA Ops:
  0.0 1.1 %copy-start.2 = (bf16[512,512]{1,0:T(8,128)(2,1)S(1)}, bf16[512,512]{1,0:T(8,128)(2,1)}, u32[]{:S(2)}) copy-start(bf16[512,512]{1,0:T(8,128)(2,1)} %wq_ref.1) | copy-start | bytes 1572868
  0.0 1.1 %copy-start.8 = (s32[1,1,4]{2,1,0:T(1,128)S(1)}, s32[1,1,4]{2,1,0:T(1,128)}, u32[]{:S(2)}) copy-start(s32[1,1,4]{2,1,0:T(1,128)} %param.12) | copy-start | bytes 52
  1.1 1.2 %copy-start = (bf16[512,1024]{1,0:T(8,128)(2,1)S(1)}, bf16[512,1024]{1,0:T(8,128)(2,1)}, u32[]{:S(2)}) copy-start(bf16[512,1024]{1,0:T(8,128)(2,1)} %wup_ref.1) | copy-start | bytes 3145732
  2.4 1.2 %copy-start.1 = (bf16[1024,512]{1,0:T(8,128)(2,1)S(1)}, bf16[1024,512]{1,0:T(8,128)(2,1)}, u32[]{:S(2)}) copy-start(bf16[1024,512]{1,0:T(8,128)(2,1)} %wdown_ref.1) | copy-start | bytes 3145732
  3.6 1.0 %copy-start.3 = (bf16[512,512]{1,0:T(8,128)(2,1)S(1)}, bf16[512,512]{1,0:T(8,128)(2,1)}, u32[]{:S(2)}) copy-start(bf16[512,512]{1,0:T(8,128)(2,1)} %wk_ref.1) | copy-start | bytes 1572868
  4.6 1.0 %copy-start.4 = (bf16[512,512]{1,0:T(8,128)(2,1)S(1)}, bf16[512,512]{1,0:T(8,128)(2,1)}, u32[]{:S(2)}) copy-start(bf16[512,512]{1,0:T(8,128)(2,1)} %wv_ref.1) | copy-start | bytes 1572868
  5.7 1.0 %copy-start.5 = (bf16[512,512]{1,0:T(8,128)(2,1)S(1)}, bf16[512,512]{1,0:T(8,128)(2,1)}, u32[]{:S(2)}) copy-start(bf16[512,512]{1,0:T(8,128)(2,1)} %wout_ref.1) | copy-start | bytes 1572868
  6.7 0.7 %copy-start.6 = (f32[5,512]{1,0:T(8,128)S(1)}, f32[5,512]{1,0:T(8,128)}, u32[]{:S(2)}) copy-start(f32[5,512]{1,0:T(8,128)} %conv_ref.1) | copy-start | bytes 30724
  7.4 0.7 %copy-start.7 = (f32[1024]{0:T(1024)S(1)}, f32[1024]{0:T(1024)}, u32[]{:S(2)}) copy-start(f32[1024]{0:T(1024)} %param.11) | copy-start | bytes 12292

commit v2 on v1

--- a/solution.py
+++ b/solution.py
@@ -116,9 +116,9 @@
     n_ctx,
     frame,
     mask_ref,
-    tokens_ref,
-    gain_ref,
-    conv_ref,
+    tokens_hbm,
+    gain_hbm,
+    conv_hbm,
     wq_ref,
     wk_ref,
     wv_ref,
@@ -126,6 +126,8 @@
     wout_ref,
     wdown_ref,
     out_ref,
+    gain_ref,
+    conv_ref,
     tok_all,
     normed,
     halo,
@@ -162,7 +164,7 @@
     c = lax.axis_index("ctx")
     i = lax.axis_index("tm")
     j = lax.axis_index("tp")
-    rows, width = tokens_ref.shape
+    rows, width = tokens_hbm.shape
     half_rows = rows // 2
     depth = wq_ref.shape[0]
     part = depth // 2
@@ -247,9 +249,11 @@
     ]
     local.append(
         pltpu.make_async_copy(
-            tokens_ref, tok_all.at[rows_at(c * rows, rows)], local_sem.at[6]
-        )
-    )
+            tokens_hbm, tok_all.at[rows_at(c * rows, rows)], local_sem.at[6]
+        )
+    )
+    local.append(pltpu.make_async_copy(gain_hbm, gain_ref, local_sem.at[7]))
+    local.append(pltpu.make_async_copy(conv_hbm, conv_ref, local_sem.at[8]))
     for copy in local:
         copy.start()
     pl.semaphore_wait(barrier, n_ctx + 2)
@@ -273,7 +277,7 @@
         for index, (source, target) in enumerate(slices(g, 1, 1 - i))
     ]
     halo_copy = remote(
-        tokens_ref.at[rows_at((1 - i) * (rows - 16), 16)],
+        tokens_hbm.at[rows_at((1 - i) * (rows - 16), 16)],
         halo,
         halo_sem.at[0],
         halo_sem.at[1],
@@ -287,7 +291,7 @@
     for step in range(1, n_ctx):
         peer = {"ctx": ahead(step)}
         at = step - 1
-        own_half = tokens_ref.at[rows_at(j * half_rows, half_rows)]
+        own_half = tokens_hbm.at[rows_at(j * half_rows, half_rows)]
         tok_out.append(
             remote(own_half, token_half(c, j), tok_send.at[at], tok_recv.at[at], peer)
         )
@@ -314,26 +318,17 @@
             remote(bias.at[source], bias.at[source], bias_send.at[at], bias_recv.at[at], peer)
         )
 
-    def y_regions(half):
-        other = 1 - i
+    def y_copies(half):
         return [
-            w_in.at[rows_at(other * depth + half * part, part), 0 : 3 * hw],
-            w_in.at[rows_at(other * depth + half * part, part), 3 * hw : 3 * hw + fw],
-            w_back.at[rows_at(half * (hw // 2), hw // 2), cols_at(other * cols, cols)],
-            w_back.at[rows_at(hw + half * (fw // 2), fw // 2), cols_at(other * cols, cols)],
+            remote(target, target, y_send.at[index], y_recv.at[index], to_y)
+            for index, (_, target) in enumerate(slices(half, 1, 1 - i))
         ]
 
-    y_out = [
-        remote(region, region, y_send.at[index], y_recv.at[index], to_y)
-        for index, region in enumerate(y_regions(g))
-    ]
-    y_in = [
-        remote(region, region, y_send.at[index], y_recv.at[index], to_y)
-        for index, region in enumerate(y_regions(1 - g))
-    ]
-
-    for copy in tok_out:
-        copy.start()
+    y_out, y_in = y_copies(g), y_copies(1 - g)
+
+    steps = [2, 1] + list(range(3, n_ctx))
+    for step in steps:
+        tok_out[step - 1].start()
     for copy in x_out[:4]:
         copy.start()
     halo_copy.start()
@@ -342,6 +337,7 @@
     for copy in bias_out:
         copy.start()
 
+    local[7].wait()
     gain = gain_ref[...]
 
     def norm_block(block):
@@ -351,41 +347,32 @@
     local[6].wait()
     norm_block(c)
 
-    tok_in[0].wait_recv()
-    fwd_out[0].start()
-    for copy in x_in[:3]:
-        copy.wait_recv()
-    y_out[0].start()
-    for at in range(1, n_ctx - 1):
-        tok_in[at].wait_recv()
-        fwd_out[at].start()
-        fwd_in[at - 1].wait_recv()
-        norm_block(behind(at))
-    x_in[3].wait_recv()
-    y_out[1].start()
-    fwd_in[n_ctx - 2].wait_recv()
-    norm_block(behind(n_ctx - 1))
-
-    for copy in local[:4]:
-        copy.wait()
-    y_in[0].wait_recv()
-
-    @pl.loop(0, n_ctx)
-    def _(block):
+    def pass_on(index):
+        x_in[index].wait_recv()
+        y_out[index].start()
+
+    def share(step):
+        tok_in[step - 1].wait_recv()
+        fwd_out[step - 1].start()
+
+    def settle(step):
+        fwd_in[step - 1].wait_recv()
+        norm_block(behind(step))
+
+    def project(block):
         at = rows_at(block * rows, rows)
         qkv[at, :] = jnp.dot(
             normed[at, :], w_in[:, 0 : 3 * hw], preferred_element_type=jnp.float32
         ).astype(jnp.bfloat16)
 
-    x_in[4].wait_recv()
-    y_out[2].start()
-    x_in[5].wait_recv()
-    y_out[3].start()
-    for copy in bias_in:
-        copy.wait_recv()
-
-    @pl.loop(0, n_ctx)
-    def _(block):
+    def feed(block):
+        at = rows_at(block * rows, rows)
+        hidden = jnp.dot(
+            normed[at, :], w_in[:, 3 * hw : 3 * hw + fw], preferred_element_type=jnp.float32
+        )
+        feats[at, hw : hw + fw] = jax.nn.gelu(hidden, approximate=True).astype(jnp.bfloat16)
+
+    def attend(block):
         at = rows_at(block * rows, rows)
         outs = []
         for head in range(heads):
@@ -406,42 +393,45 @@
             outs.append(mixed / total)
         feats[at, 0:hw] = jnp.concatenate(outs, axis=1).astype(jnp.bfloat16)
 
-    y_in[1].wait_recv()
-
-    @pl.loop(0, n_ctx)
-    def _(block):
-        at = rows_at(block * rows, rows)
-        hidden = jnp.dot(
-            normed[at, :], w_in[:, 3 * hw : 3 * hw + fw], preferred_element_type=jnp.float32
-        )
-        feats[at, hw : hw + fw] = jax.nn.gelu(hidden, approximate=True).astype(jnp.bfloat16)
-
+    pass_on(0)
+    pass_on(1)
+    pass_on(2)
+    share(steps[0])
+    pass_on(3)
+    share(steps[1])
+    settle(steps[0])
+    for copy in local[:4]:
+        copy.wait()
+    for copy in y_in[:3]:
+        copy.wait_recv()
+    project(c)
+    pass_on(4)
+    project(behind(steps[0]))
+    settle(steps[1])
+    project(behind(steps[1]))
+    y_in[3].wait_recv()
+    feed(c)
+    pass_on(5)
+    for step in steps[2:]:
+        share(step)
+    feed(behind(steps[0]))
+    feed(behind(steps[1]))
+    for step in steps[2:]:
+        settle(step)
+        project(behind(step))
+        feed(behind(step))
+    for copy in bias_in:
+        copy.wait_recv()
     for copy in local[4:6]:
         copy.wait()
-    y_in[2].wait_recv()
-    y_in[3].wait_recv()
-
-    order = list(range(1, n_ctx)) + [0]
-    sib_out, sib_in = [], []
-    for index, step in enumerate(order):
+
+    order = steps + [0]
+    sib, red = [], []
+
+    def reduce(index):
+        step = order[index]
         at = rows_at(ahead(step) * rows, rows)
-        copy = remote(
-            theirs.at[at], sibling.at[at], sib_send.at[index], sib_recv.at[index], to_tp
-        )
-        sib_out.append(copy)
-        theirs[at, :] = jnp.dot(
-            feats[at, :], w_back[:, cols_at((1 - j) * cols, cols)], preferred_element_type=jnp.float32
-        ).astype(jnp.bfloat16)
-        copy.start()
-    for index, step in enumerate(order):
-        at = rows_at(ahead(step) * rows, rows)
-        mine[at, :] = jnp.dot(
-            feats[at, :], w_back[:, cols_at(j * cols, cols)], preferred_element_type=jnp.float32
-        )
-    red = []
-    for index, step in enumerate(order[:-1]):
-        at = rows_at(ahead(step) * rows, rows)
-        sib_out[index].wait_recv()
+        sib[index].wait_recv()
         summed[step - 1] = (mine[at, :] + sibling[at, :].astype(jnp.float32)).astype(jnp.bfloat16)
         copy = remote(
             summed.at[step - 1],
@@ -453,6 +443,28 @@
         copy.start()
         red.append(copy)
 
+    for index, step in enumerate(order):
+        block = ahead(step)
+        at = rows_at(block * rows, rows)
+        attend(block)
+        if index == 0:
+            y_in[4].wait_recv()
+            y_in[5].wait_recv()
+        theirs[at, :] = jnp.dot(
+            feats[at, :], w_back[:, cols_at((1 - j) * cols, cols)], preferred_element_type=jnp.float32
+        ).astype(jnp.bfloat16)
+        copy = remote(
+            theirs.at[at], sibling.at[at], sib_send.at[index], sib_recv.at[index], to_tp
+        )
+        copy.start()
+        sib.append(copy)
+        mine[at, :] = jnp.dot(
+            feats[at, :], w_back[:, cols_at(j * cols, cols)], preferred_element_type=jnp.float32
+        )
+        if index < n_ctx - 1:
+            reduce(index)
+
+    local[8].wait()
     halo_copy.wait_recv()
     halo_normed[...] = normalised(halo[...], gain)
     edge = halo_normed[:, cols_at(j * cols, cols)].astype(jnp.float32)
@@ -464,11 +476,11 @@
     extended[0:8, :] = before
     extended[8 : 8 + rows, :] = normed[own, my_cols].astype(jnp.float32)
     extended[8 + rows : 16 + rows, :] = after
-    base = tokens_ref[:, my_cols].astype(jnp.float32)
+    base = tok_all[own, my_cols].astype(jnp.float32)
     for tap in range(KERNEL):
         shift = 8 + (tap - reach) * frame
         base = base + conv_ref[tap : tap + 1, :] * extended[shift : shift + rows, :]
-    sib_out[n_ctx - 1].wait_recv()
+    sib[n_ctx - 1].wait_recv()
     base = base + mine[own, :] + sibling[own, :].astype(jnp.float32)
     for copy in red:
         copy.wait_recv()
@@ -476,7 +488,7 @@
         base = base + arrived[step].astype(jnp.float32)
     out_ref[...] = base.astype(out_ref.dtype)
 
-    for copy in tok_out + x_out + [halo_copy] + bias_out + fwd_out + y_out + sib_out + red:
+    for copy in tok_out + x_out + [halo_copy] + bias_out + fwd_out + y_out + sib + red:
         copy.wait_send()
 
 
@@ -497,9 +509,11 @@
     out = pl.pallas_call(
         functools.partial(layer_kernel, n_ctx, dancers_here),
         out_shape=jax.ShapeDtypeStruct((rows, cols), bf16),
-        in_specs=[pl.BlockSpec(memory_space=pltpu.SMEM)] + [vmem] * 3 + [hbm] * 6,
+        in_specs=[pl.BlockSpec(memory_space=pltpu.SMEM)] + [hbm] * 9,
         out_specs=vmem,
         scratch_shapes=[
+            pltpu.VMEM((1, width), f32),
+            pltpu.VMEM(conv_weight.shape, f32),
             pltpu.VMEM((every, width), bf16),
             pltpu.VMEM((every, width), bf16),
             pltpu.VMEM((16, width), bf16),
@@ -515,7 +529,7 @@
             pltpu.VMEM((n_ctx - 1, rows, cols), bf16),
             pltpu.VMEM((n_ctx - 1, rows, cols), bf16),
             pltpu.VMEM((rows + 16, cols), f32),
-            dma((7,)),
+            dma((9,)),
             dma((n_ctx - 1,)),
             dma((n_ctx - 1,)),
             dma((n_ctx - 1,)),
@@ -524,8 +538,8 @@
             dma((n_ctx - 1,)),
             dma((6,)),
             dma((6,)),
-            dma((4,)),
-            dma((4,)),
+            dma((6,)),
+            dma((6,)),
             dma((2,)),
             dma((n_ctx,)),
             dma((n_ctx,)),
@@ -533,7 +547,7 @@
             dma((n_ctx - 1,)),
         ],
         compiler_params=pltpu.CompilerParams(
-            collective_id=0, has_side_effects=True, vmem_limit_bytes=40 << 20
+            collective_id=0, has_side_effects=True, vmem_limit_bytes=60 * 1024 * 1024
         ),
     )(
         block_mask[0],

time: 51.6 us -> 44.6 us (0.86)
  local copies, waits for them, and re-layouts: 8.8 us -> 3.35 us
  Pallas kernels: 42.3 us -> 41.1 us
    unnamed x18 -> x0, local copies, waits for them, and re-layouts: 6.98 us -> none
    pallas_call x1, Pallas kernels: 42.3 us -> 41.1 us  [in_one_kernel(): pl.pallas_call(functools.partial(layer_kernel, n_ctx, dancers_here), out_...]
    reshape x1, local copies, waits for them, and re-layouts: 0.71 us -> 1.62 us  [in_one_kernel(): return out.reshape(frames_here, dancers_here, cols)]
    reshape x1, local copies, waits for them, and re-layouts: 1.11 us -> 1.74 us  [in_one_kernel(): tokens.reshape(rows, width)]
where the time goes in v2:
time: 44.6 us; the launch traced here: 44.5 us
  Pallas kernels  41.1 us (92%)
  local copies, waits for them, and re-layouts  3.35 us (8%)
    pallas_call x1, Pallas kernels, in_one_kernel(): pl.pallas_call(functools.partial(layer_kernel, n_ctx, dancers_here), out_...  41.1 us
    reshape x1, local copies, waits for them, and re-layouts, in_one_kernel(): tokens.reshape(rows, width)  1.74 us
    reshape x1, local copies, waits for them, and re-layouts, in_one_kernel(): return out.reshape(frames_here, dancers_here, cols)  1.62 us

profile of v2, /device:TPU:0, one launch (start us, length us, event | category | flops | bytes accessed | tf_op | source)
XLA Modules:
  0.0 44.5 jit_solution(7838357747298025125)
XLA Ops:
  0.0 1.7 %reshape.6.tokens_hbm = bf16[128,1024]{1,0:T(8,128)(2,1)} reshape(bf16[64,2,1024]{2,1,0:T(2,128)(2,1)} %param.10) | data formatting | bytes 524288 | tf_op jit(solution)/shard_map/reshape | solution.py:554
  1.7 41.1 %shard_map.100 = bf16[128,512]{1,0:T(8,128)(2,1)} custom-call(s32[1,4]{1,0:T(1,128)} %bitcast.3, bf16[128,1024]{1,0:T(8,128)(2,1)} %reshape.6.tokens_hbm, f32[1,1024]{1,0:T(1,128)} %bitcast.2, f32[5,512]{1,0:T(8,128)} %conv_hbm.1, bf16[512,512]{1,0:T(8,128)(2,1)} %wq_ref.1, bf16[512,512]{1,0:T(8,128)(2,1)} %wk_ref.1, bf16[512,512]{1,0:T(8,128)(2,1)} %wv_ref.1, ...), custom_call_target="tpu_custom_call" | custom-call | tf_op jit(solution)/shard_map/pallas_call | solution.py:509
  42.9 1.6 %reshape.7 = bf16[64,2,512]{2,1,0:T(2,128)(2,1)} reshape(bf16[128,512]{1,0:T(8,128)(2,1)} %shard_map.100) | data formatting | bytes 262144 | tf_op jit(solution)/shard_map/reshape | solution.py:564

commit v3 on v2

--- a/solution.py
+++ b/solution.py
@@ -427,42 +427,70 @@
 
     order = steps + [0]
     sib, red = [], []
+    for index, step in enumerate(order):
+        at = rows_at(ahead(step) * rows, rows)
+        sib.append(
+            remote(theirs.at[at], sibling.at[at], sib_send.at[index], sib_recv.at[index], to_tp)
+        )
+        if step > 0:
+            red.append(
+                remote(
+                    summed.at[step - 1],
+                    arrived.at[step - 1],
+                    red_send.at[step - 1],
+                    red_recv.at[step - 1],
+                    {"ctx": ahead(step)},
+                )
+            )
+
+    def product(index, half):
+        at = rows_at(ahead(order[index]) * rows, rows)
+        return jnp.dot(
+            feats[at, :], w_back[:, cols_at(half * cols, cols)], preferred_element_type=jnp.float32
+        )
+
+    def give(index, half):
+        at = rows_at(ahead(order[index]) * rows, rows)
+        theirs[at, :] = product(index, half).astype(jnp.bfloat16)
+        sib[index].start()
+
+    def keep(index, half):
+        at = rows_at(ahead(order[index]) * rows, rows)
+        mine[at, :] = product(index, half)
 
     def reduce(index):
         step = order[index]
         at = rows_at(ahead(step) * rows, rows)
         sib[index].wait_recv()
         summed[step - 1] = (mine[at, :] + sibling[at, :].astype(jnp.float32)).astype(jnp.bfloat16)
-        copy = remote(
-            summed.at[step - 1],
-            arrived.at[step - 1],
-            red_send.at[step - 1],
-            red_recv.at[step - 1],
-            {"ctx": ahead(step)},
-        )
-        copy.start()
-        red.append(copy)
+        red[index].start()
 
     for index, step in enumerate(order):
-        block = ahead(step)
-        at = rows_at(block * rows, rows)
-        attend(block)
-        if index == 0:
-            y_in[4].wait_recv()
-            y_in[5].wait_recv()
-        theirs[at, :] = jnp.dot(
-            feats[at, :], w_back[:, cols_at((1 - j) * cols, cols)], preferred_element_type=jnp.float32
-        ).astype(jnp.bfloat16)
-        copy = remote(
-            theirs.at[at], sibling.at[at], sib_send.at[index], sib_recv.at[index], to_tp
-        )
-        copy.start()
-        sib.append(copy)
-        mine[at, :] = jnp.dot(
-            feats[at, :], w_back[:, cols_at(j * cols, cols)], preferred_element_type=jnp.float32
-        )
-        if index < n_ctx - 1:
-            reduce(index)
+        attend(ahead(step))
+
+        @pl.when(j != i)
+        def _(index=index):
+            give(index, i)
+
+        @pl.when(j == i)
+        def _(index=index):
+            keep(index, i)
+            if index > 0:
+                reduce(index - 1)
+
+    y_in[4].wait_recv()
+    y_in[5].wait_recv()
+    for index in range(n_ctx):
+
+        @pl.when(j == i)
+        def _(index=index):
+            give(index, 1 - i)
+
+        @pl.when(j != i)
+        def _(index=index):
+            keep(index, 1 - i)
+            if index > 0:
+                reduce(index - 1)
 
     local[8].wait()
     halo_copy.wait_recv()

time: 44.6 us -> 41.8 us (0.937)
  Pallas kernels: 41.1 us -> 38.3 us
    pallas_call x1, Pallas kernels: 41.1 us -> 38.3 us  [in_one_kernel(): pl.pallas_call(functools.partial(layer_kernel, n_ctx, dancers_here), out_...]
where the time goes in v3:
time: 41.8 us; the launch traced here: 41.7 us
  Pallas kernels  38.3 us (92%)
  local copies, waits for them, and re-layouts  3.35 us (8%)
    pallas_call x1, Pallas kernels, in_one_kernel(): pl.pallas_call(functools.partial(layer_kernel, n_ctx, dancers_here), out_...  38.3 us
    reshape x1, local copies, waits for them, and re-layouts, in_one_kernel(): tokens.reshape(rows, width)  1.74 us
    reshape x1, local copies, waits for them, and re-layouts, in_one_kernel(): return out.reshape(frames_here, dancers_here, cols)  1.62 us

profile of v3, /device:TPU:0, one launch (start us, length us, event | category | flops | bytes accessed | tf_op | source)
XLA Modules:
  0.0 41.7 jit_solution(11249700089566972087)
XLA Ops:
  0.0 1.7 %reshape.6.tokens_hbm = bf16[128,1024]{1,0:T(8,128)(2,1)} reshape(bf16[64,2,1024]{2,1,0:T(2,128)(2,1)} %param.10) | data formatting | bytes 524288 | tf_op jit(solution)/shard_map/reshape | solution.py:582
  1.7 38.3 %shard_map.100 = bf16[128,512]{1,0:T(8,128)(2,1)} custom-call(s32[1,4]{1,0:T(1,128)} %bitcast.3, bf16[128,1024]{1,0:T(8,128)(2,1)} %reshape.6.tokens_hbm, f32[1,1024]{1,0:T(1,128)} %bitcast.2, f32[5,512]{1,0:T(8,128)} %conv_hbm.1, bf16[512,512]{1,0:T(8,128)(2,1)} %wq_ref.1, bf16[512,512]{1,0:T(8,128)(2,1)} %wk_ref.1, bf16[512,512]{1,0:T(8,128)(2,1)} %wv_ref.1, ...), custom_call_target="tpu_custom_call" | custom-call | tf_op jit(solution)/shard_map/pallas_call | solution.py:537
  40.1 1.6 %reshape.7 = bf16[64,2,512]{2,1,0:T(2,128)(2,1)} reshape(bf16[128,512]{1,0:T(8,128)(2,1)} %shard_map.100) | data formatting | bytes 262144 | tf_op jit(solution)/shard_map/reshape | solution.py:592

commit v4 on v3

--- a/solution.py
+++ b/solution.py
@@ -232,15 +232,15 @@
                 ],
             )
         )
-        out.append(
-            (
-                wdown_ref.at[rows_at(c * fw + first * (fw // 2), count * (fw // 2)), :],
-                w_back.at[
-                    rows_at(hw + first * (fw // 2), count * (fw // 2)),
-                    cols_at(owner * cols, cols),
-                ],
-            )
-        )
+        quarter = count * (fw // 2) // 2
+        for piece in range(2):
+            start = first * (fw // 2) + piece * quarter
+            out.append(
+                (
+                    wdown_ref.at[rows_at(c * fw + start, quarter), :],
+                    w_back.at[rows_at(hw + start, quarter), cols_at(owner * cols, cols)],
+                )
+            )
         return out
 
     local = [
@@ -249,11 +249,11 @@
     ]
     local.append(
         pltpu.make_async_copy(
-            tokens_hbm, tok_all.at[rows_at(c * rows, rows)], local_sem.at[6]
-        )
-    )
-    local.append(pltpu.make_async_copy(gain_hbm, gain_ref, local_sem.at[7]))
-    local.append(pltpu.make_async_copy(conv_hbm, conv_ref, local_sem.at[8]))
+            tokens_hbm, tok_all.at[rows_at(c * rows, rows)], local_sem.at[7]
+        )
+    )
+    local.append(pltpu.make_async_copy(gain_hbm, gain_ref, local_sem.at[8]))
+    local.append(pltpu.make_async_copy(conv_hbm, conv_ref, local_sem.at[9]))
     for copy in local:
         copy.start()
     pl.semaphore_wait(barrier, n_ctx + 2)
@@ -337,14 +337,14 @@
     for copy in bias_out:
         copy.start()
 
-    local[7].wait()
+    local[8].wait()
     gain = gain_ref[...]
 
     def norm_block(block):
         at = rows_at(block * rows, rows)
         normed[at, :] = normalised(tok_all[at, :], gain)
 
-    local[6].wait()
+    local[7].wait()
     norm_block(c)
 
     def pass_on(index):
@@ -411,18 +411,19 @@
     project(behind(steps[1]))
     y_in[3].wait_recv()
     feed(c)
-    pass_on(5)
     for step in steps[2:]:
         share(step)
+    pass_on(5)
     feed(behind(steps[0]))
     feed(behind(steps[1]))
     for step in steps[2:]:
         settle(step)
         project(behind(step))
         feed(behind(step))
+    pass_on(6)
     for copy in bias_in:
         copy.wait_recv()
-    for copy in local[4:6]:
+    for copy in local[4:7]:
         copy.wait()
 
     order = steps + [0]
@@ -480,6 +481,7 @@
 
     y_in[4].wait_recv()
     y_in[5].wait_recv()
+    y_in[6].wait_recv()
     for index in range(n_ctx):
 
         @pl.when(j == i)
@@ -492,7 +494,7 @@
             if index > 0:
                 reduce(index - 1)
 
-    local[8].wait()
+    local[9].wait()
     halo_copy.wait_recv()
     halo_normed[...] = normalised(halo[...], gain)
     edge = halo_normed[:, cols_at(j * cols, cols)].astype(jnp.float32)
@@ -557,17 +559,17 @@
             pltpu.VMEM((n_ctx - 1, rows, cols), bf16),
             pltpu.VMEM((n_ctx - 1, rows, cols), bf16),
             pltpu.VMEM((rows + 16, cols), f32),
-            dma((9,)),
-            dma((n_ctx - 1,)),
-            dma((n_ctx - 1,)),
-            dma((n_ctx - 1,)),
-            dma((n_ctx - 1,)),
-            dma((n_ctx - 1,)),
-            dma((n_ctx - 1,)),
-            dma((6,)),
-            dma((6,)),
-            dma((6,)),
-            dma((6,)),
+            dma((10,)),
+            dma((n_ctx - 1,)),
+            dma((n_ctx - 1,)),
+            dma((n_ctx - 1,)),
+            dma((n_ctx - 1,)),
+            dma((n_ctx - 1,)),
+            dma((n_ctx - 1,)),
+            dma((7,)),
+            dma((7,)),
+            dma((7,)),
+            dma((7,)),
             dma((2,)),
             dma((n_ctx,)),
             dma((n_ctx,)),

time: 41.8 us -> 42 us (level)
  no operation moved by 1% of the time
where the time goes in v4:
time: 42 us; the launch traced here: 41.8 us
  Pallas kernels  38.4 us (91%)
  local copies, waits for them, and re-layouts  3.35 us (8%)
    pallas_call x1, Pallas kernels, in_one_kernel(): pl.pallas_call(functools.partial(layer_kernel, n_ctx, dancers_here), out_...  38.4 us
    reshape x1, local copies, waits for them, and re-layouts, in_one_kernel(): tokens.reshape(rows, width)  1.74 us
    reshape x1, local copies, waits for them, and re-layouts, in_one_kernel(): return out.reshape(frames_here, dancers_here, cols)  1.62 us

profile of v4, /device:TPU:0, one launch (start us, length us, event | category | flops | bytes accessed | tf_op | source)
XLA Modules:
  0.0 41.8 jit_solution(2026028541557958057)
XLA Ops:
  0.0 1.7 %reshape.6.tokens_hbm = bf16[128,1024]{1,0:T(8,128)(2,1)} reshape(bf16[64,2,1024]{2,1,0:T(2,128)(2,1)} %param.10) | data formatting | bytes 524288 | tf_op jit(solution)/shard_map/reshape | solution.py:584
  1.7 38.4 %shard_map.100 = bf16[128,512]{1,0:T(8,128)(2,1)} custom-call(s32[1,4]{1,0:T(1,128)} %bitcast.3, bf16[128,1024]{1,0:T(8,128)(2,1)} %reshape.6.tokens_hbm, f32[1,1024]{1,0:T(1,128)} %bitcast.2, f32[5,512]{1,0:T(8,128)} %conv_hbm.1, bf16[512,512]{1,0:T(8,128)(2,1)} %wq_ref.1, bf16[512,512]{1,0:T(8,128)(2,1)} %wk_ref.1, bf16[512,512]{1,0:T(8,128)(2,1)} %wv_ref.1, ...), custom_call_target="tpu_custom_call" | custom-call | tf_op jit(solution)/shard_map/pallas_call | solution.py:539
  40.2 1.6 %reshape.7 = bf16[64,2,512]{2,1,0:T(2,128)(2,1)} reshape(bf16[128,512]{1,0:T(8,128)(2,1)} %shard_map.100) | data formatting | bytes 262144 | tf_op jit(solution)/shard_map/reshape | solution.py:594
